TPU v7x, 32 devices: a whole 2x2x4 slice. The times are simulated.
32 devices in a mesh: section: 4 (over y, core), shard: 2 (over x), tensor: 4 (over z).
Axes of the slice: x: 2, y: 2, z: 4, core: 2. Of those that a mesh axis runs over, the one named last changes fastest.
Arguments:
- gradient: bfloat16 [48, 2560, 1024], P('section', ('shard', 'tensor')), may hold values from -15000 to 15000
- momentum: float32 [48, 2560, 1024], P('section', ('shard', 'tensor')), may hold values from -28000 to 28000
- weight: bfloat16 [48, 2560, 1024], P('section', ('shard', 'tensor')), may hold values from -0.1875 to 0.1875
Outputs:
- new_weight: bfloat16 [48, 2560, 1024], P('section', ('shard', 'tensor'))
- new_momentum: float32 [48, 2560, 1024], P('section', ('shard', 'tensor'))
- update: bfloat16 [48, 2560, 1024], P('section', ('shard', 'tensor'))
All inputs are finite; a program needn't handle non-finite values.
Results may differ from a plain program's by a relative error of at most 0.029.
Values may be sent and summed in bfloat16 or wider, within the bound.
A program may use at most 256 MiB of HBM per device.

v0:
```python
import math
import jax
import jax.numpy as jnp
from jax import lax
from jax.sharding import PartitionSpec as P

D = 1024
HID = 2560
ITERS = 3
decay_rate = 0.95
epsilon = 1e-07
coeff_one = 3.4445
coeff_two = -4.775
coeff_three = 2.0315
learn_rate = 0.02
weight_decay = 0.1


def shortened(x):

    def short(part):
        return part.astype(jnp.bfloat16) if part.dtype == jnp.float32 else part

    return jax.tree.map(short, x)


def gram_matrix(partial_value):
    return lax.psum(partial_value.astype(jnp.bfloat16), "tensor").astype(jnp.float32)


def orthogonalize(nesterov):
    values = nesterov.astype(jnp.float32)
    total = lax.psum(jnp.sum(values * values, axis=(1, 2)), "tensor")
    current = (values / (jnp.sqrt(total)[:, None, None] + epsilon)).astype(jnp.bfloat16)
    for iteration in range(ITERS):
        partial_value = jnp.einsum(
            "krd,kre->kde", current, current, preferred_element_type=jnp.float32
        )
        gram = gram_matrix(partial_value)
        gram_bf = gram.astype(jnp.bfloat16)
        squared = jnp.einsum("kde,kef->kdf", gram_bf, gram_bf, preferred_element_type=jnp.float32)
        mixer = (coeff_two * gram + coeff_three * squared).astype(jnp.bfloat16)
        mixed = jnp.einsum("krd,kde->kre", current, mixer, preferred_element_type=jnp.float32)
        current = (coeff_one * current.astype(jnp.float32) + mixed).astype(jnp.bfloat16)
    update_gain = 0.2 * math.sqrt(max(HID, D))
    return (update_gain * current.astype(jnp.float32)).astype(jnp.bfloat16)


def apply_update(weight, update):
    weight_values = weight.astype(jnp.float32)
    return (
        weight_values - learn_rate * (update.astype(jnp.float32) + weight_decay * weight_values)
    ).astype(jnp.bfloat16)


def pad_slots(values, padded_count):
    extra = padded_count - values.shape[0]
    if extra == 0:
        return values
    filler = jnp.zeros((extra,) + values.shape[1:], values.dtype)
    return jnp.concatenate([values, filler], axis=0)


def local(gradient, momentum, weight):
    section_mats = gradient.shape[0]
    shards = lax.axis_size("shard")
    slot_count = (section_mats + shards - 1) // shards
    padded_count = slot_count * shards
    grad_dealt, weight_dealt = (
        lax.all_to_all(
            pad_slots(gradient, padded_count), "shard", split_axis=0, concat_axis=1, tiled=True
        ),
        lax.all_to_all(
            pad_slots(weight, padded_count), "shard", split_axis=0, concat_axis=1, tiled=True
        ),
    )
    moment_dealt = lax.all_to_all(
        pad_slots(momentum, padded_count).astype(jnp.bfloat16),
        "shard",
        split_axis=0,
        concat_axis=1,
        tiled=True,
    ).astype(jnp.float32)
    grad_values = grad_dealt.astype(jnp.float32)
    new_momentum = decay_rate * moment_dealt + grad_values
    nesterov = (grad_values + decay_rate * new_momentum).astype(jnp.bfloat16)
    update = orthogonalize(nesterov)
    new_weight = apply_update(weight_dealt, update)
    back_weight, back_update = (
        lax.all_to_all(new_weight, "shard", split_axis=1, concat_axis=0, tiled=True),
        lax.all_to_all(update, "shard", split_axis=1, concat_axis=0, tiled=True),
    )
    back_moment = lax.all_to_all(
        shortened(new_momentum), "shard", split_axis=1, concat_axis=0, tiled=True
    ).astype(new_momentum.dtype)
    return (back_weight[:section_mats], back_moment[:section_mats], back_update[:section_mats])


def solution(mesh):
    return jax.shard_map(
        local,
        mesh=mesh,
        in_specs=(
            P("section", ("shard", "tensor"), None),
            P("section", ("shard", "tensor"), None),
            P("section", ("shard", "tensor"), None),
        ),
        out_specs=(
            P("section", ("shard", "tensor"), None),
            P("section", ("shard", "tensor"), None),
            P("section", ("shard", "tensor"), None),
        ),
        check_vma=False,
    )
```

profile of v0, /device:TPU:0, one launch (start us, length us, event | category | flops | bytes accessed | tf_op | source)
XLA Modules:
  0.0 1968.1 jit_solution(14599514388412769811)
XLA Ops:
  7.2 9.9 convert_element_type.139
  17.1 98.9 %all_to_all.72 = bf16[12,320,1024]{2,1,0:T(8,128)(2,1)} all-to-all(bf16[12,320,1024]{2,1,0:T(8,128)(2,1)} %convert_element_type.139), channel_id=1, replica_groups=mesh['section'=4,'shard'=2,'tensor'=4] {'shard'}, dimensions={0} | all-to-all | bytes 15728640 | tf_op jit(solution)/shard_map/all_to_all | solution.py:77
  116.0 6.8 all-to-all-start.1
  122.8 0.0 all-reduce.4.cloned.1.call-start
  122.8 11.3 convert_multiply_fusion
  134.2 14.5 copy.17
  148.6 60.6 %all-to-all-done.1 = bf16[12,320,1024]{2,1,0:T(8,128)(2,1)} async-done(((bf16[12,320,1024]{2,1,0:T(8,128)(2,1)}), bf16[12,320,1024]{2,1,0:T(8,128)(2,1)}, u32[]{:S(2)}, u32[]{:S(2)}) %all-to-all-start.1) | async-done | bytes 7864352 | tf_op jit(solution)/shard_map/all_to_all | solution.py:70
  209.2 9.2 multiply_reduce_fusion
  218.4 11.1 copy.16
  229.5 12.1 psum.28
  241.6 16.3 fusion.22
  257.9 17.3 convolution_convert_fusion.2
  275.2 0.0 all-reduce.4.cloned.1.call-update
  275.2 0.6 all-reduce.6.cloned.1.call-start
  275.8 423.0 %all-reduce.4.cloned.1.call-done = bf16[6,1024,1024]{2,1,0:T(8,128)(2,1)} async-done(((bf16[6,1024,1024]{2,1,0:T(8,128)(2,1)}), bf16[6,1024,1024]{2,1,0:T(8,128)(2,1)}) %all-reduce.4.cloned.1.call-update) | async-done | bytes 12582928 | tf_op jit(solution)/shard_map/psum | solution.py:28
  698.8 35.4 %add_convert_fusion.5 = bf16[6,640,1024]{2,1,0:T(8,128)(2,1)} fusion(bf16[6,640,1024]{2,1,0:T(8,128)(2,1)} %get-tuple-element.4, bf16[6,1024,1024]{2,1,0:T(8,128)(2,1)} %all-reduce.4.cloned.1.call-done), kind=kOutput, calls=%fused_computation.19 | convolution fusion | flops 20985151488 | bytes 28311552 | tf_op jit(solution)/shard_map/krd,kde->kre/dot_general | solution.py:43
  734.2 17.3 convolution_convert_fusion.1
  751.5 0.0 all-reduce.6.cloned.1.call-update
  751.5 0.2 all-reduce.8.cloned.1.call-start
  751.7 425.0 %all-reduce.6.cloned.1.call-done = bf16[6,1024,1024]{2,1,0:T(8,128)(2,1)} async-done(((bf16[6,1024,1024]{2,1,0:T(8,128)(2,1)}), bf16[6,1024,1024]{2,1,0:T(8,128)(2,1)}) %all-reduce.6.cloned.1.call-update) | async-done | bytes 12582928 | tf_op jit(solution)/shard_map/psum | solution.py:28
  1176.7 35.2 %add_convert_fusion.4 = bf16[6,640,1024]{2,1,0:T(8,128)(2,1)} fusion(bf16[6,640,1024]{2,1,0:T(8,128)(2,1)} %add_convert_fusion.5, bf16[6,1024,1024]{2,1,0:T(8,128)(2,1)} %all-reduce.6.cloned.1.call-done), kind=kOutput, calls=%fused_computation.18 | convolution fusion | flops 20985151488 | bytes 28311552 | tf_op jit(solution)/shard_map/krd,kde->kre/dot_general | solution.py:43
  1211.9 17.2 convolution_convert_fusion
  1229.1 0.0 all-reduce.8.cloned.1.call-update
  1229.1 91.7 %all_to_all.73 = bf16[12,320,1024]{2,1,0:T(8,128)(2,1)S(1)} all-to-all(bf16[12,320,1024]{2,1,0:T(8,128)(2,1)} %param.5), channel_id=1, replica_groups=mesh['section'=4,'shard'=2,'tensor'=4] {'shard'}, dimensions={0} | all-to-all | bytes 15728640 | tf_op jit(solution)/shard_map/all_to_all | solution.py:73
  1320.8 7.8 copy.15
  1328.6 12.0 copy.23
  1340.6 8.1 all-to-all-start.4
  1348.7 305.6 %all-reduce.8.cloned.1.call-done = bf16[6,1024,1024]{2,1,0:T(8,128)(2,1)} async-done(((bf16[6,1024,1024]{2,1,0:T(8,128)(2,1)}), bf16[6,1024,1024]{2,1,0:T(8,128)(2,1)}) %all-reduce.8.cloned.1.call-update) | async-done | bytes 12582928 | tf_op jit(solution)/shard_map/psum | solution.py:28
  1654.3 38.6 %fusion.2 = (bf16[6,640,1024]{2,1,0:T(8,128)(2,1)}, bf16[6,640,1024]{2,1,0:T(8,128)(2,1)}) fusion(f32[2,6,320,1024]{3,2,0,1:T(8,128)} %copy.15, bf16[6,640,1024]{2,1,0:T(8,128)(2,1)} %add_convert_fusion.4, bf16[6,1024,1024]{2,1,0:T(8,128)(2,1)} %all-reduce.8.cloned.1.call-done), kind=kOutput, calls=%fused_computation.9 | convolution fusion | flops 21020540928 | bytes 51904512 | tf_op jit(solution)/shard_map/krd,kde->kre/dot_general | solution.py:43
  1692.9 12.0 copy.21
  1704.9 0.0 all-to-all-done.4
  1704.9 7.9 all-to-all-start.3
  1712.8 11.8 copy.25
  1724.7 103.2 %all-to-all-done.3 = bf16[6,640,1024]{2,0,1:T(8,128)(2,1)} async-done(((bf16[6,640,1024]{2,0,1:T(8,128)(2,1)}), bf16[6,640,1024]{2,0,1:T(8,128)(2,1)}, u32[]{:S(2)}, u32[]{:S(2)}) %all-to-all-start.3) | async-done | bytes 7864352 | tf_op jit(solution)/shard_map/all_to_all | solution.py:90
  1827.9 7.6 all-to-all-start.5
  1835.6 13.9 convert_bitcast_fusion
  1849.4 17.9 copy.24
  1867.3 11.6 copy.22
  1878.9 70.9 %all-to-all-done.5 = bf16[6,640,1024]{2,0,1:T(8,128)(2,1)} async-done(((bf16[6,640,1024]{2,0,1:T(8,128)(2,1)}), bf16[6,640,1024]{2,0,1:T(8,128)(2,1)}, u32[]{:S(2)}, u32[]{:S(2)}) %all-to-all-start.5) | async-done | bytes 7864352 | tf_op jit(solution)/shard_map/all_to_all | solution.py:91
  1949.8 11.6 copy.26
  (1 shorter events, 0.0 us)
Async XLA Ops:
  116.0 93.2 %all-to-all-start.1 = ((bf16[12,320,1024]{2,1,0:T(8,128)(2,1)}), bf16[12,320,1024]{2,1,0:T(8,128)(2,1)}, u32[]{:S(2)}, u32[]{:S(2)}) async-start(bf16[12,320,1024]{2,1,0:T(8,128)(2,1)} %param.3), calls=%async_computation.1 | async-start | bytes 15728640 | tf_op jit(solution)/shard_map/all_to_all | solution.py:70
  122.8 576.0 %all-reduce.4.cloned.1.call-start = ((), (), s32[]{:S(2)}) async-start(), calls=%async_computation.6 | async-start | bytes 25165824 | tf_op jit(solution)/shard_map/psum | solution.py:28
  275.2 901.5 %all-reduce.6.cloned.1.call-start = ((), (), s32[]{:S(2)}) async-start(), calls=%async_computation.7 | async-start | bytes 25165824 | tf_op jit(solution)/shard_map/psum | solution.py:28
  751.5 902.8 %all-reduce.8.cloned.1.call-start = ((), (), s32[]{:S(2)}) async-start(), calls=%async_computation.8 | async-start | bytes 25165824 | tf_op jit(solution)/shard_map/psum | solution.py:28
  1340.6 364.3 %all-to-all-start.4 = ((bf16[6,640,1024]{2,0,1:T(8,128)(2,1)}), bf16[6,640,1024]{2,0,1:T(8,128)(2,1)}, u32[]{:S(2)}, u32[]{:S(2)}) async-start(bf16[6,640,1024]{2,0,1:T(8,128)(2,1)} %copy.23), calls=%async_computation.4 | async-start | bytes 20971520 | tf_op jit(solution)/shard_map/all_to_all | solution.py:93
  1704.9 123.0 %all-to-all-start.3 = ((bf16[6,640,1024]{2,0,1:T(8,128)(2,1)}), bf16[6,640,1024]{2,0,1:T(8,128)(2,1)}, u32[]{:S(2)}, u32[]{:S(2)}) async-start(bf16[6,640,1024]{2,0,1:T(8,128)(2,1)} %copy.21), calls=%async_computation.3 | async-start | bytes 20971520 | tf_op jit(solution)/shard_map/all_to_all | solution.py:90
  1827.9 121.9 %all-to-all-start.5 = ((bf16[6,640,1024]{2,0,1:T(8,128)(2,1)}), bf16[6,640,1024]{2,0,1:T(8,128)(2,1)}, u32[]{:S(2)}, u32[]{:S(2)}) async-start(bf16[6,640,1024]{2,0,1:T(8,128)(2,1)} %copy.25), calls=%async_computation.5 | async-start | bytes 20971520 | tf_op jit(solution)/shard_map/all_to_all | solution.py:91
Sparse Core Ops, SparseCore 0:
  275.3 423.3 all-reduce.3
  751.6 425.0 all-reduce.5
  1229.2 425.0 all-reduce.7
where the time goes:
time: 1980 us; the launch traced here: 1970 us
  waiting for transfers between devices  1390 us (70%)
  blocking collectives  203 us (10%)
  matrix products  161 us (8%)
  local copies, waits for them, and re-layouts  110 us (6%)
  other arithmetic  60.6 us (3%)
  starting transfers between devices  31.2 us (2%)
    psum x3, waiting for transfers between devices, gram_matrix(): lax.psum(partial_value.astype(jnp.bfloat16), 'tensor').astype(jnp.float32)  1150 us
    dot_general x3, matrix products, orthogonalize(): jnp.einsum('krd,kde->kre', current, mixer, preferred_element_type=jnp.flo...  109 us
    all_to_all x1, waiting for transfers between devices, local(): lax.all_to_all(new_weight, 'shard', split_axis=1, concat_axis=0, tiled=True)  103 us
    all_to_all x1, blocking collectives, local(): lax.all_to_all(pad_slots(momentum, padded_count).astype(jnp.bfloat16), 's...  98.9 us
    all_to_all x1, blocking collectives, local(): lax.all_to_all(pad_slots(weight, padded_count), 'shard', split_axis=0, co...  91.7 us
    all_to_all x1, waiting for transfers between devices, local(): lax.all_to_all(update, 'shard', split_axis=1, concat_axis=0, tiled=True)  70.9 us
    all_to_all x1, waiting for transfers between devices, local(): lax.all_to_all(pad_slots(gradient, padded_count), 'shard', split_axis=0,...  60.6 us
    dot_general x3, matrix products, orthogonalize(): jnp.einsum('krd,kre->kde', current, current, preferred_element_type=jnp.f...  51.8 us
  transfers between devices with their start and end apart: 7, of which 6 were waited for; matrix products, arithmetic and copies ran while one was open for 8% of the time, Pallas kernels for 0%

commit v1 on v0

--- a/solution.py
+++ b/solution.py
@@ -25,7 +25,8 @@
 
 
 def gram_matrix(partial_value):
-    return lax.psum(partial_value.astype(jnp.bfloat16), "tensor").astype(jnp.float32)
+    register_record = lambda panel, dev_axis: lax.all_gather(panel, dev_axis).sum(axis=0)
+    return register_record(partial_value.astype(jnp.bfloat16), "tensor").astype(jnp.float32)
 
 
 def orthogonalize(nesterov):

time: 1980 us -> 3280 us (1.66)
  waiting for transfers between devices: 1390 us -> 2620 us
  other arithmetic: 60.6 us -> 132 us
    all_gather x0 -> x3, waiting for transfers between devices: none -> 2380 us  [gram_matrix(): lax.all_gather(panel, dev_axis).sum(axis=0)]
    psum x3 -> x0, waiting for transfers between devices: 1150 us -> none  [gram_matrix(): lax.psum(partial_value.astype(jnp.bfloat16), 'tensor').astype(jnp.float32)]
    reduce_sum x0 -> x3, other arithmetic: none -> 71.6 us  [gram_matrix(): lax.all_gather(panel, dev_axis).sum(axis=0)]
  transfers between devices with their start and end apart: 7 -> 7, of which waited for: 6 -> 6; matrix products, arithmetic and copies ran while one was open for 8% -> 5% of each run, Pallas kernels for 0% -> 0%
where the time goes in v1:
time: 3280 us; the launch traced here: 3270 us
  waiting for transfers between devices  2620 us (80%)
  blocking collectives  203 us (6%)
  matrix products  162 us (5%)
  other arithmetic  132 us (4%)
  local copies, waits for them, and re-layouts  110 us (3%)
    all_gather x3, waiting for transfers between devices, gram_matrix(): lax.all_gather(panel, dev_axis).sum(axis=0)  2380 us
    dot_general x3, matrix products, orthogonalize(): jnp.einsum('krd,kde->kre', current, mixer, preferred_element_type=jnp.flo...  109 us
    all_to_all x1, waiting for transfers between devices, local(): lax.all_to_all(new_weight, 'shard', split_axis=1, concat_axis=0, tiled=True)  104 us
    all_to_all x1, blocking collectives, local(): lax.all_to_all(pad_slots(momentum, padded_count).astype(jnp.bfloat16), 's...  98.9 us
    all_to_all x1, blocking collectives, local(): lax.all_to_all(pad_slots(weight, padded_count), 'shard', split_axis=0, co...  91.9 us
    reduce_sum x3, other arithmetic, gram_matrix(): lax.all_gather(panel, dev_axis).sum(axis=0)  71.6 us
    all_to_all x1, waiting for transfers between devices, local(): lax.all_to_all(update, 'shard', split_axis=1, concat_axis=0, tiled=True)  71.1 us
  transfers between devices with their start and end apart: 7, of which 6 were waited for; matrix products, arithmetic and copies ran while one was open for 5% of the time, Pallas kernels for 0%

profile of v1, /device:TPU:0, one launch (start us, length us, event | category | flops | bytes accessed | tf_op | source)
XLA Modules:
  0.0 3269.4 jit_solution(15132391458741290272)
XLA Ops:
  7.2 9.9 convert_element_type.145
  17.1 98.9 %all_to_all.72 = bf16[12,320,1024]{2,1,0:T(8,128)(2,1)} all-to-all(bf16[12,320,1024]{2,1,0:T(8,128)(2,1)} %convert_element_type.145), channel_id=1, replica_groups=mesh['section'=4,'shard'=2,'tensor'=4] {'shard'}, dimensions={0} | all-to-all | bytes 15728640 | tf_op jit(solution)/shard_map/all_to_all | solution.py:78
  116.0 6.8 all-to-all-start.1
  122.8 0.0 all-gather.7.cloned.1.call-start
  122.8 11.3 convert_multiply_fusion
  134.2 14.5 copy.17
  148.7 60.5 %all-to-all-done.1 = bf16[12,320,1024]{2,1,0:T(8,128)(2,1)} async-done(((bf16[12,320,1024]{2,1,0:T(8,128)(2,1)}), bf16[12,320,1024]{2,1,0:T(8,128)(2,1)}, u32[]{:S(2)}, u32[]{:S(2)}) %all-to-all-start.1) | async-done | bytes 7864352 | tf_op jit(solution)/shard_map/all_to_all | solution.py:71
  209.2 9.2 multiply_reduce_fusion
  218.4 11.1 copy.16
  229.5 12.0 psum.7
  241.5 16.3 fusion.22
  257.8 17.6 convolution_convert_fusion.2
  275.4 0.0 all-gather.7.cloned.1.call-update
  275.4 0.0 all-gather.9.cloned.1.call-start
  275.5 833.4 %all-gather.7.cloned.1.call-done = bf16[24,1024,1024]{2,1,0:T(8,128)(2,1)} async-done(((bf16[6,1024,1024]{2,1,0:T(8,128)(2,1)}), bf16[24,1024,1024]{2,1,0:T(8,128)(2,1)}) %all-gather.7.cloned.1.call-update) | async-done | bytes 50331664 | tf_op jit(solution)/shard_map/all_gather | solution.py:28
  1108.9 23.9 reduce_sum.46
  1132.8 35.5 %add_convert_fusion.5 = bf16[6,640,1024]{2,1,0:T(8,128)(2,1)} fusion(bf16[6,640,1024]{2,1,0:T(8,128)(2,1)} %get-tuple-element.4, bf16[6,1024,1024]{2,1,0:T(8,128)(2,1)} %reduce_sum.46), kind=kOutput, calls=%fused_computation.19 | convolution fusion | flops 20985151488 | bytes 28311552 | tf_op jit(solution)/shard_map/krd,kde->kre/dot_general | solution.py:44
  1168.3 17.3 convolution_convert_fusion.1
  1185.6 0.0 all-gather.9.cloned.1.call-update
  1185.6 0.0 all-gather.11.cloned.1.call-start
  1185.6 834.3 %all-gather.9.cloned.1.call-done = bf16[24,1024,1024]{2,1,0:T(8,128)(2,1)} async-done(((bf16[6,1024,1024]{2,1,0:T(8,128)(2,1)}), bf16[24,1024,1024]{2,1,0:T(8,128)(2,1)}) %all-gather.9.cloned.1.call-update) | async-done | bytes 50331664 | tf_op jit(solution)/shard_map/all_gather | solution.py:28
  2019.9 24.1 reduce_sum.47
  2044.0 35.3 %add_convert_fusion.4 = bf16[6,640,1024]{2,1,0:T(8,128)(2,1)} fusion(bf16[6,640,1024]{2,1,0:T(8,128)(2,1)} %add_convert_fusion.5, bf16[6,1024,1024]{2,1,0:T(8,128)(2,1)} %reduce_sum.47), kind=kOutput, calls=%fused_computation.18 | convolution fusion | flops 20985151488 | bytes 28311552 | tf_op jit(solution)/shard_map/krd,kde->kre/dot_general | solution.py:44
  2079.4 17.5 convolution_convert_fusion
  2096.9 0.0 all-gather.11.cloned.1.call-update
  2096.9 91.9 %all_to_all.73 = bf16[12,320,1024]{2,1,0:T(8,128)(2,1)S(1)} all-to-all(bf16[12,320,1024]{2,1,0:T(8,128)(2,1)} %param.5), channel_id=1, replica_groups=mesh['section'=4,'shard'=2,'tensor'=4] {'shard'}, dimensions={0} | all-to-all | bytes 15728640 | tf_op jit(solution)/shard_map/all_to_all | solution.py:74
  2188.8 7.8 copy.15
  2196.6 11.9 copy.23
  2208.5 7.7 all-to-all-start.4
  2216.2 715.1 %all-gather.11.cloned.1.call-done = bf16[24,1024,1024]{2,1,0:T(8,128)(2,1)} async-done(((bf16[6,1024,1024]{2,1,0:T(8,128)(2,1)}), bf16[24,1024,1024]{2,1,0:T(8,128)(2,1)}) %all-gather.11.cloned.1.call-update) | async-done | bytes 50331664 | tf_op jit(solution)/shard_map/all_gather | solution.py:28
  2931.3 23.6 reduce_sum.48
  2954.9 38.7 %fusion.2 = (bf16[6,640,1024]{2,1,0:T(8,128)(2,1)}, bf16[6,640,1024]{2,1,0:T(8,128)(2,1)}) fusion(f32[2,6,320,1024]{3,2,0,1:T(8,128)} %copy.15, bf16[6,640,1024]{2,1,0:T(8,128)(2,1)} %add_convert_fusion.4, bf16[6,1024,1024]{2,1,0:T(8,128)(2,1)} %reduce_sum.48), kind=kOutput, calls=%fused_computation.9 | convolution fusion | flops 21020540928 | bytes 51904512 | tf_op jit(solution)/shard_map/krd,kde->kre/dot_general | solution.py:44
  2993.5 12.0 copy.21
  3005.5 0.0 all-to-all-done.4
  3005.5 8.1 all-to-all-start.3
  3013.6 11.7 copy.25
  3025.3 103.6 %all-to-all-done.3 = bf16[6,640,1024]{2,0,1:T(8,128)(2,1)} async-done(((bf16[6,640,1024]{2,0,1:T(8,128)(2,1)}), bf16[6,640,1024]{2,0,1:T(8,128)(2,1)}, u32[]{:S(2)}, u32[]{:S(2)}) %all-to-all-start.3) | async-done | bytes 7864352 | tf_op jit(solution)/shard_map/all_to_all | solution.py:91
  3128.9 7.7 all-to-all-start.5
  3136.6 13.9 convert_bitcast_fusion
  3150.5 17.8 copy.24
  3168.3 11.6 copy.22
  3179.9 71.1 %all-to-all-done.5 = bf16[6,640,1024]{2,0,1:T(8,128)(2,1)} async-done(((bf16[6,640,1024]{2,0,1:T(8,128)(2,1)}), bf16[6,640,1024]{2,0,1:T(8,128)(2,1)}, u32[]{:S(2)}, u32[]{:S(2)}) %all-to-all-start.5) | async-done | bytes 7864352 | tf_op jit(solution)/shard_map/all_to_all | solution.py:92
  3251.1 11.6 copy.26
  (1 shorter events, 0.0 us)
Async XLA Ops:
  116.0 93.2 %all-to-all-start.1 = ((bf16[12,320,1024]{2,1,0:T(8,128)(2,1)}), bf16[12,320,1024]{2,1,0:T(8,128)(2,1)}, u32[]{:S(2)}, u32[]{:S(2)}) async-start(bf16[12,320,1024]{2,1,0:T(8,128)(2,1)} %param.3), calls=%async_computation.1 | async-start | bytes 15728640 | tf_op jit(solution)/shard_map/all_to_all | solution.py:71
  122.8 986.1 %all-gather.7.cloned.1.call-start = ((), (), s32[]{:S(2)}) async-start(), calls=%async_computation.6 | async-start | bytes 62914560 | tf_op jit(solution)/shard_map/all_gather | solution.py:28
  275.4 1744.5 %all-gather.9.cloned.1.call-start = ((), (), s32[]{:S(2)}) async-start(), calls=%async_computation.7 | async-start | bytes 62914560 | tf_op jit(solution)/shard_map/all_gather | solution.py:28
  1185.6 1745.7 %all-gather.11.cloned.1.call-start = ((), (), s32[]{:S(2)}) async-start(), calls=%async_computation.8 | async-start | bytes 62914560 | tf_op jit(solution)/shard_map/all_gather | solution.py:28
  2208.5 797.0 %all-to-all-start.4 = ((bf16[6,640,1024]{2,0,1:T(8,128)(2,1)}), bf16[6,640,1024]{2,0,1:T(8,128)(2,1)}, u32[]{:S(2)}, u32[]{:S(2)}) async-start(bf16[6,640,1024]{2,0,1:T(8,128)(2,1)} %copy.23), calls=%async_computation.4 | async-start | bytes 20971520 | tf_op jit(solution)/shard_map/all_to_all | solution.py:94
  3005.5 123.4 %all-to-all-start.3 = ((bf16[6,640,1024]{2,0,1:T(8,128)(2,1)}), bf16[6,640,1024]{2,0,1:T(8,128)(2,1)}, u32[]{:S(2)}, u32[]{:S(2)}) async-start(bf16[6,640,1024]{2,0,1:T(8,128)(2,1)} %copy.21), calls=%async_computation.3 | async-start | bytes 20971520 | tf_op jit(solution)/shard_map/all_to_all | solution.py:91
  3128.9 122.2 %all-to-all-start.5 = ((bf16[6,640,1024]{2,0,1:T(8,128)(2,1)}), bf16[6,640,1024]{2,0,1:T(8,128)(2,1)}, u32[]{:S(2)}, u32[]{:S(2)}) async-start(bf16[6,640,1024]{2,0,1:T(8,128)(2,1)} %copy.25), calls=%async_computation.5 | async-start | bytes 20971520 | tf_op jit(solution)/shard_map/all_to_all | solution.py:92
Sparse Core Ops, SparseCore 0:
  275.5 833.2 all-gather.6
  1185.7 834.1 all-gather.8
  2097.0 834.1 all-gather.10
